TPU v7x, 512 devices: a whole 4x4x16 slice. The times are simulated.
512 devices in a mesh: dst: 128 (over z, x, core), src: 4 (over y).
Axes of the slice: x: 4, y: 4, z: 16, core: 2. Of those that a mesh axis runs over, the one named last changes fastest.
Arguments:
- query_rows: bfloat16 [131072, 512], P('dst'), may hold values from -1000 to 1000
- key_rows: bfloat16 [131072, 512], P(('dst', 'src')), may hold values from -12 to 12
- value_rows: bfloat16 [131072, 512], P(('dst', 'src')), may hold values from -6 to 6
- out_grad: bfloat16 [131072, 512], P('dst'), may hold values from -6 to 6
- node_labels: int32 [131072], replicated, may hold values from 0 to 3, as said below
- tile_list: int32 [512, 10], P(('dst', 'src')), may hold values from 0 to 19, as said below
- tile_count: int32 [512], P(('dst', 'src')), may hold values from 1 to 10
Outputs:
- query_grad: bfloat16 [131072, 512], P(('dst', 'src'))
- key_grad: bfloat16 [131072, 512], P(('dst', 'src'))
- value_grad: bfloat16 [131072, 512], P(('dst', 'src'))
Inputs may be any that keep to these rules, and one draw needn't show every extreme that they name: `node_labels`: nodes 2m and 2m + 1 carry the same label. `tile_list`: row d holds distinct entries t * 5 + b with 0 <= d // 4 + b - 2 < 128; its first entry is (d % 4) * 5 + 2.
All inputs are finite; a program needn't handle non-finite values.
Results may differ from a plain program's by a relative error of at most 0.015.
Values may be sent and summed in bfloat16 or wider, within the bound.
A program may use at most 64 MiB of HBM per device.

v0:
```python
import functools
import math

import jax
import jax.numpy as jnp
from jax import lax
from jax.experimental import pallas as pl
from jax.experimental.pallas import tpu as pltpu
from jax.sharding import PartitionSpec as P

HEAD_DIM = 64
REACH = 2
BAND = 5
QUARTERS = 4
TILE = 256
LANES = 128
MASKED = -(2.0**100)
WARMTH = 0.125
TO_LOG2 = WARMTH * math.log2(math.e)
OFFSETS = (2, -2, 1, -1)
MESH = pl.DeviceIdType.MESH

NT = (((1,), (1,)), ((), ()))
NN = (((1,), (0,)), ((), ()))


def dot(a, b, dims):
    return lax.dot_general(a, b, dims, preferred_element_type=jnp.float32)


def kernel(groups, chunks, maxt, *refs):
    refs = list(refs)

    def take(n):
        got, refs[:] = refs[:n], refs[n:]
        return got

    tl, tc, q_in, k_in, v_in, g_in, lab_in = take(7)
    q_out, k_out, v_out = take(3)
    q_v, g_v = take(chunks), take(chunks)
    k_v, v_v = take(chunks), take(chunks)
    lab_q, lab_k, q_hot, k_hot, k_t = take(5)
    p_v, d_v = take(2), take(2)
    st_v = take(2)
    fin_v, dq_c, dk_c, dv_c = take(4)
    st_send, st_recv = take(2)
    kv_send, kv_recv, kv_own = take(3)
    dq_send, dq_recv, dq_own = take(3)
    inv, = take(1)
    load_sem, lab_sem, kv_ss, kv_rs, st_ss, st_rs, gr_ss, gr_rs, dq_ss, dq_rs = take(10)

    me = lax.axis_index("dst")
    quarter = lax.axis_index("src")

    def dst_peer(offset):
        return (lax.rem(me + offset + groups, groups), quarter)

    def src_peer(step):
        return (me, lax.rem(quarter + step, QUARTERS))

    lanes_of = lambda c: pl.ds(c * LANES, LANES)

    loads = []
    for c in range(chunks):
        own = []
        for n, (src, dst) in enumerate(
            (
                (k_in.at[:, lanes_of(c)], k_v[c].at[REACH]),
                (v_in.at[:, lanes_of(c)], v_v[c].at[REACH]),
                (q_in.at[:, :, lanes_of(c)], q_v[c]),
                (g_in.at[:, :, lanes_of(c)], g_v[c]),
            )
        ):
            copy = pltpu.make_async_copy(src, dst, load_sem.at[c, n])
            copy.start()
            own.append(copy)
        loads.append(own)
    lab_loads = []
    for b in range(BAND):
        group = lax.rem(me + (b - REACH) + groups, groups)
        copy = pltpu.make_async_copy(
            lab_in.at[pl.ds(group * 8, 8)], lab_k.at[b], lab_sem.at[b]
        )
        copy.start()
        lab_loads.append(copy)
    copy = pltpu.make_async_copy(lab_in.at[pl.ds(me * 8, 8)], lab_q, lab_sem.at[BAND])
    copy.start()
    lab_loads.append(copy)

    barrier = pltpu.get_barrier_semaphore()
    for offset in OFFSETS:
        pl.semaphore_signal(barrier, inc=1, device_id=dst_peer(offset), device_id_type=MESH)
    for step in range(1, QUARTERS):
        pl.semaphore_signal(barrier, inc=1, device_id=src_peer(step), device_id_type=MESH)
    pl.semaphore_wait(barrier, len(OFFSETS) + QUARTERS - 1)

    gathers = []
    for c in range(chunks):
        sent = []
        for n, offset in enumerate(OFFSETS):
            for m, (src, dst) in enumerate(((k_in, k_v[c]), (v_in, v_v[c]))):
                copy = pltpu.make_async_remote_copy(
                    src_ref=src.at[:, lanes_of(c)],
                    dst_ref=dst.at[REACH - offset],
                    send_sem=kv_ss.at[c, n, m],
                    recv_sem=kv_rs.at[c, n, m],
                    device_id=dst_peer(offset),
                    device_id_type=MESH,
                )
                copy.start()
                sent.append(copy)
        gathers.append(sent)

    count = tc[0]
    for t in range(QUARTERS):
        for b in range(BAND):
            at = jnp.int32(maxt)
            for i in range(maxt):
                hit = jnp.logical_and(tl[0, i] == t * BAND + b, i < count)
                at = jnp.where(hit, jnp.int32(i), at)
            inv[t * BAND + b] = at

    for copy in lab_loads:
        copy.wait()
    level = lax.broadcasted_iota(jnp.int32, (LANES, LANES), 0)
    for t in range(QUARTERS):
        for half in range(TILE // LANES):
            row = lab_q[pl.ds(2 * t + half, 1), :]
            hot = jnp.where(level == row, 1.0, 0.0)
            q_hot[t, pl.ds(half * LANES, LANES), :] = hot.T.astype(jnp.bfloat16)
    for b in range(BAND):
        for half in range(TILE // LANES):
            row = lab_k[b, pl.ds(2 * quarter + half, 1), :]
            hot = jnp.where(level == row, 0.0, MASKED)
            k_hot[b, pl.ds(half * LANES, LANES), :] = hot.T.astype(jnp.bfloat16)

    for ref in (dq_c, dk_c, dv_c):
        ref[maxt] = jnp.zeros(ref.shape[1:], ref.dtype)
    for ref in st_v:
        ref[maxt, pl.ds(0, 2), :] = jnp.full((2, TILE), MASKED, jnp.float32)
        ref[maxt, pl.ds(2, 6), :] = jnp.zeros((6, TILE), jnp.float32)

    first = lax.broadcasted_iota(jnp.int32, (TILE, LANES), 1) < HEAD_DIM

    def stacked(x):
        zero = jnp.zeros_like(x)
        return jnp.concatenate([jnp.where(first, x, zero), jnp.where(first, zero, x)], 0)

    def entry(i):
        code = tl[0, i]
        t = lax.div(code, jnp.int32(BAND))
        return t, code - t * BAND

    def score_pass(c):
        for copy in loads[c]:
            copy.wait()
        for copy in gathers[c]:
            copy.wait_recv()
        half = c % 2

        @pl.loop(0, BAND)
        def _(b):
            k_t[half, b] = k_v[c][b].astype(jnp.float32).T.astype(jnp.bfloat16)

        @pl.loop(0, maxt)
        def _(i):
            t, b = entry(i)
            k = stacked(k_v[c][b])
            hot = k_hot[b]
            left = jnp.concatenate([k, jnp.concatenate([hot, hot], 0)], 1)
            right = jnp.concatenate([q_v[c][t], q_hot[t]], 1)
            scores = dot(left, right, NT)
            grads = dot(stacked(v_v[c][b]), g_v[c][t], NT)
            for h in range(2):
                rows = slice(h * TILE, (h + 1) * TILE)
                s, g = scores[rows], grads[rows]
                top = jnp.max(s, axis=0, keepdims=True)
                p = jnp.exp2((s - top) * TO_LOG2)
                st_v[half][i, pl.ds(h, 1), :] = top
                st_v[half][i, pl.ds(2 + h, 1), :] = jnp.sum(p, axis=0, keepdims=True)
                st_v[half][i, pl.ds(4 + h, 1), :] = jnp.sum(p * g, axis=0, keepdims=True)
                p_v[half][i, pl.ds(h * TILE, TILE), :] = p
                d_v[half][i, pl.ds(h * TILE, TILE), :] = g

        for t in range(QUARTERS):
            at = [inv[t * BAND + b] for b in range(BAND)]
            tops = [st_v[half][a, pl.ds(0, 2), :] for a in at]
            top = functools.reduce(jnp.maximum, tops)
            total = jnp.zeros_like(top)
            delta = jnp.zeros_like(top)
            for a, one in zip(at, tops):
                scale = jnp.exp2((one - top) * TO_LOG2)
                total = total + st_v[half][a, pl.ds(2, 2), :] * scale
                delta = delta + st_v[half][a, pl.ds(4, 2), :] * scale
            for n, value in enumerate((top, total, delta)):
                st_send[c, n, pl.ds(2 * t, 2), :] = value
        sent = []
        for step in range(1, QUARTERS):
            copy = pltpu.make_async_remote_copy(
                src_ref=st_send.at[c],
                dst_ref=st_recv.at[c, step - 1],
                send_sem=st_ss.at[c, step - 1],
                recv_sem=st_rs.at[c, step - 1],
                device_id=src_peer(step),
                device_id_type=MESH,
            )
            copy.start()
            sent.append(copy)
        return sent

    def grad_pass(c, stats):
        half = c % 2
        for copy in stats:
            copy.wait_recv()
        parts = [st_send.at[c]] + [st_recv.at[c, n] for n in range(QUARTERS - 1)]
        tops = [part[0] for part in parts]
        top = functools.reduce(jnp.maximum, tops)
        total = jnp.zeros_like(top)
        delta = jnp.zeros_like(top)
        for part, one in zip(parts, tops):
            scale = jnp.exp2((one - top) * TO_LOG2)
            total = total + part[1] * scale
            delta = delta + part[2] * scale
        each = 1.0 / total
        delta = delta / total
        for t in range(QUARTERS):
            for n, value in enumerate((top, each, delta)):
                fin_v[t, pl.ds(2 * n, 2), :] = value[2 * t : 2 * t + 2]

        @pl.loop(0, maxt)
        def _(i):
            t, b = entry(i)
            probs, slopes = [], []
            for h in range(2):
                top = fin_v[t, pl.ds(h, 1), :]
                each = fin_v[t, pl.ds(2 + h, 1), :]
                delta = fin_v[t, pl.ds(4 + h, 1), :]
                own = st_v[half][i, pl.ds(h, 1), :]
                scale = jnp.exp2((own - top) * TO_LOG2) * each
                p = p_v[half][i, pl.ds(h * TILE, TILE), :] * scale
                g = d_v[half][i, pl.ds(h * TILE, TILE), :]
                probs.append(p.astype(jnp.bfloat16))
                slopes.append((p * (g - delta)).astype(jnp.bfloat16))
            dv = dot(jnp.concatenate(probs, 0), g_v[c][t], NN)
            dk = dot(jnp.concatenate(slopes, 0), q_v[c][t], NN)
            dv_c[i] = jnp.where(first, dv[:TILE], dv[TILE:])
            dk_c[i] = jnp.where(first, dk[:TILE], dk[TILE:])
            for h in range(2):
                k = k_t[half, b, pl.ds(h * HEAD_DIM, HEAD_DIM), :]
                dq_c[i, pl.ds(h * HEAD_DIM, HEAD_DIM), :] = dot(k, slopes[h], NN)

        def listed(ref, places):
            return functools.reduce(jnp.add, [ref[inv[at]] for at in places])

        sent = []
        for b in [REACH + o for o in OFFSETS] + [REACH]:
            places = [t * BAND + b for t in range(QUARTERS)]
            dk = listed(dk_c, places) * WARMTH
            dv = listed(dv_c, places)
            if b == REACH:
                kv_own[c, 0] = dk
                kv_own[c, 1] = dv
                continue
            n = OFFSETS.index(b - REACH)
            kv_send[c, n, 0] = dk.astype(jnp.bfloat16)
            kv_send[c, n, 1] = dv.astype(jnp.bfloat16)
            copy = pltpu.make_async_remote_copy(
                src_ref=kv_send.at[c, n],
                dst_ref=kv_recv.at[c, n],
                send_sem=gr_ss.at[c, n],
                recv_sem=gr_rs.at[c, n],
                device_id=dst_peer(b - REACH),
                device_id_type=MESH,
            )
            copy.start()
            sent.append(copy)
        for t in range(QUARTERS):
            dq = listed(dq_c, [t * BAND + b for b in range(BAND)]) * WARMTH
            dq_own[c, t] = dq
            dq_send[c, t] = dq.astype(jnp.bfloat16)
        for step in range(1, QUARTERS):
            copy = pltpu.make_async_remote_copy(
                src_ref=dq_send.at[c, lax.rem(quarter + step, QUARTERS)],
                dst_ref=dq_recv.at[c, step - 1],
                send_sem=dq_ss.at[c, step - 1],
                recv_sem=dq_rs.at[c, step - 1],
                device_id=src_peer(step),
                device_id_type=MESH,
            )
            copy.start()
            sent.append(copy)
        return sent

    def finish(c, sent):
        for copy in sent:
            copy.wait_recv()
        for m, out in enumerate((k_out, v_out)):
            total = kv_own[c, m]
            for n in range(len(OFFSETS)):
                total = total + kv_recv[c, n, m].astype(jnp.float32)
            out[:, lanes_of(c)] = total.astype(jnp.bfloat16)
        total = dq_own[c, quarter]
        for n in range(QUARTERS - 1):
            total = total + dq_recv[c, n].astype(jnp.float32)
        q_out[:, lanes_of(c)] = total.T.astype(jnp.bfloat16)

    stats, grads = {}, {}
    for c in range(chunks + 1):
        if c < chunks:
            stats[c] = score_pass(c)
        if c >= 1:
            grads[c - 1] = grad_pass(c - 1, stats[c - 1])
        if c >= 2:
            finish(c - 2, grads[c - 2])
    finish(chunks - 1, grads[chunks - 1])

    for sent in gathers + list(stats.values()) + list(grads.values()):
        for copy in sent:
            copy.wait_send()


def on_device(groups, query_rows, key_rows, value_rows, out_grad, node_labels, tile_list, tile_count):
    rows, width = key_rows.shape
    chunks = width // LANES
    maxt = tile_list.shape[1]
    bf16, f32 = jnp.bfloat16, jnp.float32
    vmem = pltpu.VMEM
    dma = pltpu.SemaphoreType.DMA
    near = len(OFFSETS)
    far = QUARTERS - 1
    scratch = (
        [vmem((QUARTERS, TILE, LANES), bf16)] * (2 * chunks)
        + [vmem((BAND, TILE, LANES), bf16)] * (2 * chunks)
        + [
            vmem((8, LANES), jnp.int32),
            vmem((BAND, 8, LANES), jnp.int32),
            vmem((QUARTERS, TILE, LANES), bf16),
            vmem((BAND, TILE, LANES), bf16),
            vmem((2, BAND, LANES, TILE), bf16),
        ]
        + [vmem((maxt, 2 * TILE, TILE), f32)] * 4
        + [vmem((maxt + 1, 8, TILE), f32)] * 2
        + [
            vmem((QUARTERS, 8, TILE), f32),
            vmem((maxt + 1, LANES, TILE), f32),
            vmem((maxt + 1, TILE, LANES), f32),
            vmem((maxt + 1, TILE, LANES), f32),
            vmem((chunks, 3, 8, TILE), f32),
            vmem((chunks, far, 3, 8, TILE), f32),
            vmem((chunks, near, 2, TILE, LANES), bf16),
            vmem((chunks, near, 2, TILE, LANES), bf16),
            vmem((chunks, 2, TILE, LANES), f32),
            vmem((chunks, QUARTERS, LANES, TILE), bf16),
            vmem((chunks, far, LANES, TILE), bf16),
            vmem((chunks, QUARTERS, LANES, TILE), f32),
            pltpu.SMEM((QUARTERS * BAND,), jnp.int32),
            dma((chunks, 4)),
            dma((BAND + 1,)),
            dma((chunks, near, 2)),
            dma((chunks, near, 2)),
            dma((chunks, far)),
            dma((chunks, far)),
            dma((chunks, near)),
            dma((chunks, near)),
            dma((chunks, far)),
            dma((chunks, far)),
        ]
    )
    smem = pl.BlockSpec(memory_space=pltpu.SMEM)
    anywhere = pl.BlockSpec(memory_space=pl.ANY)
    return pl.pallas_call(
        functools.partial(kernel, groups, chunks, maxt),
        out_shape=[jax.ShapeDtypeStruct((rows, width), bf16)] * 3,
        in_specs=[smem, smem] + [anywhere] * 5,
        out_specs=[pl.BlockSpec(memory_space=vmem)] * 3,
        scratch_shapes=scratch,
        compiler_params=pltpu.CompilerParams(
            collective_id=0, has_side_effects=True, vmem_limit_bytes=60 * 1024 * 1024
        ),
    )(
        tile_list,
        tile_count,
        query_rows.reshape(QUARTERS, TILE, width),
        key_rows,
        value_rows,
        out_grad.reshape(QUARTERS, TILE, width),
        node_labels.reshape(-1, LANES),
    )


def solution(mesh):
    both = P(("dst", "src"), None)
    return jax.shard_map(
        functools.partial(on_device, mesh.shape["dst"]),
        mesh=mesh,
        in_specs=(P("dst", None), both, both, P("dst", None), P(), both, P(("dst", "src"))),
        out_specs=(both, both, both),
        check_vma=False,
    )
```

profile of v0, /device:TPU:1, one launch (start us, length us, event | category | flops | bytes accessed | tf_op | source)
XLA Modules:
  0.0 72.3 jit_solution(13716950369136902704)
XLA Ops:
  1.3 67.5 %shard_map.94 = (bf16[256,512]{1,0:T(8,128)(2,1)}, bf16[256,512]{1,0:T(8,128)(2,1)}, bf16[256,512]{1,0:T(8,128)(2,1)}) custom-call(s32[1,10]{1,0:T(1,128)} %refs_0_.1, s32[1]{0:T(128)S(6)} %copy.13.refs_1_, bf16[4,256,512]{2,1,0:T(8,128)(2,1)} %bitcast.3, bf16[256,512]{1,0:T(8,128)(2,1)} %refs_3_.1, bf16[256,512]{1,0:T(8,128)(2,1)} %refs_4_.1, ...), custom_call_target="tpu_custom_call" | custom-call | tf_op jit(solution)/shard_map/pallas_call | solution.py:371
  68.8 0.0 copy-start.1
  68.8 1.7 %copy.14 = bf16[256,512]{1,0:T(8,128)(2,1)} copy(bf16[256,512]{1,0:T(8,128)(2,1)} %get-tuple-element.6) | data formatting | bytes 524288
  70.5 0.0 copy-done.1
  70.5 0.0 copy-start
  70.5 0.7 copy.15
  71.2 0.3 copy-done
  71.6 0.7 copy.16
Async XLA Ops:
  68.8 1.7 %copy-start.1 = (bf16[256,512]{1,0:T(8,128)(2,1)S(1)}, bf16[256,512]{1,0:T(8,128)(2,1)}, u32[]{:S(2)}) copy-start(bf16[256,512]{1,0:T(8,128)(2,1)} %get-tuple-element.7) | copy-start | bytes 786436
  70.5 1.0 %copy-start = (bf16[256,512]{1,0:T(8,128)(2,1)S(1)}, bf16[256,512]{1,0:T(8,128)(2,1)}, u32[]{:S(2)}) copy-start(bf16[256,512]{1,0:T(8,128)(2,1)} %get-tuple-element.8) | copy-start | bytes 786436
where the time goes:
time: 72.5 us; the launch traced here: 72.3 us
  Pallas kernels  67.5 us (93%)
  local copies, waits for them, and re-layouts  3.46 us (5%)
  between operations  1.3 us (2%)
    pallas_call x1, Pallas kernels, on_device(): pl.pallas_call(functools.partial(kernel, groups, chunks, maxt), out_shape...  67.5 us
    unnamed x7, local copies, waits for them, and re-layouts  3.46 us

commit v1 on v0

v1 whole, which is shorter than its diff:
```python
import functools
import math

import jax
import jax.numpy as jnp
from jax import lax
from jax.experimental import pallas as pl
from jax.experimental.pallas import tpu as pltpu
from jax.sharding import PartitionSpec as P

HEAD_DIM = 64
REACH = 2
BAND = 5
QUARTERS = 4
TILE = 256
LANES = 128
MASKED = -(2.0**100)
WARMTH = 0.125
TO_LOG2 = WARMTH * math.log2(math.e)
MESH = pl.DeviceIdType.MESH

NT = (((1,), (1,)), ((), ()))
NN = (((1,), (0,)), ((), ()))


def dot(a, b, dims):
    return lax.dot_general(a, b, dims, preferred_element_type=jnp.float32)


def kernel(groups, chunks, maxt, *refs):
    refs = list(refs)

    def take(n):
        got, refs[:] = refs[:n], refs[n:]
        return got

    tl, tc, q_in, k_in, v_in, g_in, lab_in = take(7)
    q_out, k_out, v_out = take(3)
    q_v, g_v = take(chunks), take(chunks)
    kv_v = take(chunks)
    lab_q, lab_k, q_hot, k_hot, k_t, q_t, g_t = take(7)
    p_v = take(2)
    s_v, pb_v, sb_v = take(2), take(2), take(2)
    v_t, = take(1)
    st_v = take(2)
    fin_v, dq_c, dk_c, dv_c = take(4)
    st_send, st_recv = take(2)
    kv_send, kv_recv, kv_mix, kv_own = take(4)
    dq_send, dq_recv, dq_own = take(3)
    inv, = take(1)
    own_sem, load_sem, lab_sem, kv_ss, kv_rs, st_ss, st_rs, gr_ss, gr_rs, dq_ss, dq_rs = take(11)

    me = lax.axis_index("dst")
    quarter = lax.axis_index("src")

    def dst_peer(offset):
        return (lax.rem(me + offset + groups, groups), quarter)

    def src_peer(step):
        return (me, lax.rem(quarter + step, QUARTERS))

    lanes_of = lambda c: pl.ds(c * LANES, LANES)

    side = 1 - 2 * lax.rem(me, 2)

    owns, loads = [], []
    for c in range(chunks):
        own = []
        for m, src in enumerate((k_in, v_in)):
            copy = pltpu.make_async_copy(
                src.at[:, lanes_of(c)], kv_v[c].at[REACH, m], own_sem.at[c, m]
            )
            copy.start()
            own.append(copy)
        owns.append(own)
    for c in range(chunks):
        own = []
        for n, (src, dst) in enumerate(((q_in, q_v[c]), (g_in, g_v[c]))):
            copy = pltpu.make_async_copy(src.at[:, :, lanes_of(c)], dst, load_sem.at[c, n])
            copy.start()
            own.append(copy)
        loads.append(own)
    lab_loads = []
    for b in range(BAND):
        group = lax.rem(me + (b - REACH) + groups, groups)
        copy = pltpu.make_async_copy(
            lab_in.at[pl.ds(group * 8, 8)], lab_k.at[b], lab_sem.at[b]
        )
        copy.start()
        lab_loads.append(copy)
    copy = pltpu.make_async_copy(lab_in.at[pl.ds(me * 8, 8)], lab_q, lab_sem.at[BAND])
    copy.start()
    lab_loads.append(copy)

    def remote(src, dst, send, recv, peer):
        copy = pltpu.make_async_remote_copy(
            src_ref=src,
            dst_ref=dst,
            send_sem=send,
            recv_sem=recv,
            device_id=peer,
            device_id_type=MESH,
        )
        copy.start()
        return copy

    peers = [dst_peer(2 * side), dst_peer(-2 * side), dst_peer(side)]
    peers += [src_peer(step) for step in range(1, QUARTERS)]
    barrier = pltpu.get_barrier_semaphore()
    for peer in peers:
        pl.semaphore_signal(barrier, inc=1, device_id=peer, device_id_type=MESH)
    pl.semaphore_wait(barrier, len(peers))

    gathers = []
    for c in range(chunks):
        for copy in owns[c]:
            copy.wait()
        gathers.append(
            [
                remote(
                    kv_v[c].at[REACH],
                    kv_v[c].at[REACH - offset],
                    kv_ss.at[c, n],
                    kv_rs.at[c, n],
                    dst_peer(offset),
                )
                for n, offset in enumerate((-2 * side, 2 * side, side))
            ]
        )

    def forward(c):
        gathers[c][0].wait_recv()
        gathers[c].append(
            remote(
                kv_v[c].at[REACH + 2 * side],
                kv_v[c].at[REACH + side],
                kv_ss.at[c, 3],
                kv_rs.at[c, 3],
                dst_peer(side),
            )
        )

    count = tc[0]
    for t in range(QUARTERS):
        for b in range(BAND):
            at = jnp.int32(maxt)
            for i in range(maxt):
                hit = jnp.logical_and(tl[0, i] == t * BAND + b, i < count)
                at = jnp.where(hit, jnp.int32(i), at)
            inv[t * BAND + b] = at

    for copy in lab_loads:
        copy.wait()
    level = lax.broadcasted_iota(jnp.int32, (LANES, LANES), 0)
    for t in range(QUARTERS):
        for half in range(TILE // LANES):
            row = lab_q[pl.ds(2 * t + half, 1), :]
            hot = jnp.where(level == row, 1.0, 0.0)
            q_hot[t, pl.ds(half * LANES, LANES), :] = hot.T.astype(jnp.bfloat16)
    for b in range(BAND):
        for half in range(TILE // LANES):
            row = lab_k[b, pl.ds(2 * quarter + half, 1), :]
            hot = jnp.where(level == row, 0.0, MASKED)
            k_hot[b, pl.ds(half * LANES, LANES), :] = hot.T.astype(jnp.bfloat16)

    for ref in (dq_c, dk_c, dv_c):
        ref[maxt] = jnp.zeros(ref.shape[1:], ref.dtype)
    for ref in st_v:
        ref[maxt, pl.ds(0, 2), :] = jnp.full((2, TILE), MASKED, jnp.float32)
        ref[maxt, pl.ds(2, 6), :] = jnp.zeros((6, TILE), jnp.float32)

    first = lax.broadcasted_iota(jnp.int32, (TILE, LANES), 1) < HEAD_DIM

    ones = jnp.ones((16, TILE), jnp.bfloat16)

    def stacked(x):
        zero = jnp.zeros_like(x)
        return jnp.concatenate([jnp.where(first, x, zero), jnp.where(first, zero, x)], 0)

    def joined(ref, h):
        rows = pl.ds(h * TILE, TILE)
        return jnp.concatenate([ref[n, rows, :] for n in range(TILE // LANES)], 1)

    def entry(i):
        code = tl[0, i]
        t = lax.div(code, jnp.int32(BAND))
        return t, code - t * BAND

    def score_pass(c):
        for copy in gathers[c][1:]:
            copy.wait_recv()
        half = c % 2

        @pl.loop(0, BAND)
        def _(b):
            k_t[half, b] = kv_v[c][b, 0].T
            v_t[b] = kv_v[c][b, 1].T

        def products(i, odd):
            t, b = entry(i)
            hot = k_hot[b]
            left = jnp.concatenate(
                [stacked(kv_v[c][b, 0]), jnp.concatenate([hot, hot], 0)], 1
            )
            right = jnp.concatenate([q_v[c][t], q_hot[t]], 1)
            s_v[odd][...] = dot(left, right, NT)

        def weigh(i, odd):
            for h in range(2):
                rows = pl.ds(h * TILE, TILE)
                for n in range(TILE // LANES):
                    lanes = pl.ds(n * LANES, LANES)
                    s = s_v[odd][rows, lanes]
                    top = jnp.max(s, axis=0, keepdims=True)
                    p = jnp.exp2((s - top) * TO_LOG2)
                    p_v[half][i, rows, lanes] = p
                    pb_v[odd][n, rows, :] = p.astype(jnp.bfloat16)
                    st_v[half][i, pl.ds(h, 1), lanes] = top

        def attend(i, odd):
            t, b = entry(i)
            for h in range(2):
                lanes = pl.ds(h * HEAD_DIM, HEAD_DIM)
                left = jnp.concatenate([v_t[b, lanes, :], ones], 0)
                out = dot(left, joined(pb_v[odd], h), NN)
                delta = out[:HEAD_DIM] * g_t[c, t, lanes, :].astype(jnp.float32)
                st_v[half][i, pl.ds(2 + h, 1), :] = out[HEAD_DIM : HEAD_DIM + 1]
                st_v[half][i, pl.ds(4 + h, 1), :] = jnp.sum(delta, axis=0, keepdims=True)

        def visit(n):
            products(2 * n + 1, 1)
            weigh(2 * n, 0)
            attend(jnp.maximum(2 * n - 1, 0), 1)
            products(jnp.minimum(2 * n + 2, maxt - 1), 0)
            weigh(2 * n + 1, 1)
            attend(2 * n, 0)

        pairs = maxt // 2
        products(0, 0)
        pl.loop(0, pairs // 2)(visit)
        if c + 1 < chunks:
            forward(c + 1)
        pl.loop(pairs // 2, pairs)(visit)
        attend(maxt - 1, 1)

        for t in range(QUARTERS):
            at = [inv[t * BAND + b] for b in range(BAND)]
            tops = [st_v[half][a, pl.ds(0, 2), :] for a in at]
            top = functools.reduce(jnp.maximum, tops)
            total = jnp.zeros_like(top)
            delta = jnp.zeros_like(top)
            for a, one in zip(at, tops):
                scale = jnp.exp2((one - top) * TO_LOG2)
                total = total + st_v[half][a, pl.ds(2, 2), :] * scale
                delta = delta + st_v[half][a, pl.ds(4, 2), :] * scale
            for n, value in enumerate((top, total, delta)):
                st_send[c, n, pl.ds(2 * t, 2), :] = value
        sent = []
        for step in range(1, QUARTERS):
            copy = pltpu.make_async_remote_copy(
                src_ref=st_send.at[c],
                dst_ref=st_recv.at[c, step - 1],
                send_sem=st_ss.at[c, step - 1],
                recv_sem=st_rs.at[c, step - 1],
                device_id=src_peer(step),
                device_id_type=MESH,
            )
            copy.start()
            sent.append(copy)
        return sent

    def grad_pass(c, stats):
        half = c % 2
        for copy in stats:
            copy.wait_recv()
        parts = [st_send.at[c]] + [st_recv.at[c, n] for n in range(QUARTERS - 1)]
        tops = [part[0] for part in parts]
        top = functools.reduce(jnp.maximum, tops)
        total = jnp.zeros_like(top)
        delta = jnp.zeros_like(top)
        for part, one in zip(parts, tops):
            scale = jnp.exp2((one - top) * TO_LOG2)
            total = total + part[1] * scale
            delta = delta + part[2] * scale
        each = 1.0 / total
        delta = delta / total
        for t in range(QUARTERS):
            for n, value in enumerate((top, each, delta)):
                fin_v[t, pl.ds(2 * n, 2), :] = value[2 * t : 2 * t + 2]

        def prob_grads(i, odd):
            t, b = entry(i)
            s_v[odd][...] = dot(stacked(kv_v[c][b, 1]), g_v[c][t], NT)

        def slopes(i, odd):
            t, _ = entry(i)
            for h in range(2):
                rows = pl.ds(h * TILE, TILE)
                for n in range(TILE // LANES):
                    lanes = pl.ds(n * LANES, LANES)
                    top = fin_v[t, pl.ds(h, 1), lanes]
                    each = fin_v[t, pl.ds(2 + h, 1), lanes]
                    delta = fin_v[t, pl.ds(4 + h, 1), lanes]
                    own = st_v[half][i, pl.ds(h, 1), lanes]
                    scale = jnp.exp2((own - top) * TO_LOG2) * each
                    p = p_v[half][i, rows, lanes] * scale
                    pb_v[odd][n, rows, :] = p.astype(jnp.bfloat16)
                    sb_v[odd][n, rows, :] = (p * (s_v[odd][rows, lanes] - delta)).astype(
                        jnp.bfloat16
                    )

        def gradients(i, odd):
            t, b = entry(i)
            for h in range(2):
                lanes = pl.ds(h * HEAD_DIM, HEAD_DIM)
                slope = joined(sb_v[odd], h)
                dv_c[i, lanes, :] = dot(g_t[c, t, lanes, :], joined(pb_v[odd], h), NT)
                dk_c[i, lanes, :] = dot(q_t[c, t, lanes, :], slope, NT)
                dq_c[i, lanes, :] = dot(k_t[half, b, lanes, :], slope, NN)

        prob_grads(0, 0)
        prob_grads(1, 1)
        slopes(0, 0)

        @pl.loop(0, maxt // 2)
        def _(n):
            after = jnp.minimum(2 * n + 2, maxt - 2)
            slopes(2 * n + 1, 1)
            prob_grads(after, 0)
            gradients(2 * n, 0)
            slopes(after, 0)
            prob_grads(after + 1, 1)
            gradients(2 * n + 1, 1)

        def listed(ref, places):
            return functools.reduce(jnp.add, [ref[inv[at]] for at in places])

        def band_sum(b):
            places = [t * BAND + b for t in range(QUARTERS)]
            return listed(dk_c, places) * WARMTH, listed(dv_c, places)

        sent = []
        for n, (b, dst, peer) in enumerate(
            (
                (REACH - side, kv_mix.at[c], side),
                (REACH - 2 * side, kv_recv.at[c, 0], -2 * side),
                (REACH + side, kv_recv.at[c, 1], side),
            )
        ):
            for m, value in enumerate(band_sum(b)):
                kv_send[c, n, m] = value.astype(jnp.bfloat16)
            sent.append(
                remote(kv_send.at[c, n], dst, gr_ss.at[c, n], gr_rs.at[c, n], dst_peer(peer))
            )
        for m, value in enumerate(band_sum(REACH)):
            kv_own[c, 0, m] = value
        for m, value in enumerate(band_sum(REACH + 2 * side)):
            kv_own[c, 1, m] = value
        for t in range(QUARTERS):
            dq = listed(dq_c, [t * BAND + b for b in range(BAND)]) * WARMTH
            dq_own[c, t] = dq
            dq_send[c, t] = dq.astype(jnp.bfloat16)
        for step in range(1, QUARTERS):
            copy = pltpu.make_async_remote_copy(
                src_ref=dq_send.at[c, lax.rem(quarter + step, QUARTERS)],
                dst_ref=dq_recv.at[c, step - 1],
                send_sem=dq_ss.at[c, step - 1],
                recv_sem=dq_rs.at[c, step - 1],
                device_id=src_peer(step),
                device_id_type=MESH,
            )
            copy.start()
            sent.append(copy)
        return sent

    def merge(c, sent):
        sent[0].wait_recv()
        for m in range(2):
            mixed = kv_own[c, 1, m] + kv_mix[c, m].astype(jnp.float32)
            kv_send[c, 3, m] = mixed.astype(jnp.bfloat16)
        sent.append(
            remote(
                kv_send.at[c, 3], kv_recv.at[c, 2], gr_ss.at[c, 3], gr_rs.at[c, 3], dst_peer(2 * side)
            )
        )

    def finish(c, sent):
        for copy in sent[1:]:
            copy.wait_recv()
        for m, out in enumerate((k_out, v_out)):
            total = kv_own[c, 0, m]
            for n in range(3):
                total = total + kv_recv[c, n, m].astype(jnp.float32)
            out[:, lanes_of(c)] = total.T.astype(jnp.bfloat16)
        total = dq_own[c, quarter]
        for n in range(QUARTERS - 1):
            total = total + dq_recv[c, n].astype(jnp.float32)
        q_out[:, lanes_of(c)] = total.T.astype(jnp.bfloat16)

    stats, grads = {}, {}
    for c in range(chunks):
        for copy in loads[c]:
            copy.wait()

        @pl.loop(0, QUARTERS)
        def _(t):
            q_t[c, t] = q_v[c][t].T
            g_t[c, t] = g_v[c][t].T

    forward(0)
    for c in range(chunks + 1):
        if c < chunks:
            stats[c] = score_pass(c)
        if c >= 2:
            merge(c - 2, grads[c - 2])
        if c >= 1:
            grads[c - 1] = grad_pass(c - 1, stats[c - 1])
        if c >= 3:
            finish(c - 3, grads[c - 3])
    finish(chunks - 2, grads[chunks - 2])
    merge(chunks - 1, grads[chunks - 1])
    finish(chunks - 1, grads[chunks - 1])

    for sent in gathers + list(stats.values()) + list(grads.values()):
        for copy in sent:
            copy.wait_send()


def handed_on(*refs):
    for src, dst in zip(refs[:3], refs[3:]):
        dst[...] = src[...]


def on_device(groups, query_rows, key_rows, value_rows, out_grad, node_labels, tile_list, tile_count):
    rows, width = key_rows.shape
    chunks = width // LANES
    maxt = tile_list.shape[1]
    bf16, f32 = jnp.bfloat16, jnp.float32
    vmem = pltpu.VMEM
    dma = pltpu.SemaphoreType.DMA
    near = 4
    far = QUARTERS - 1
    scratch = (
        [vmem((QUARTERS, TILE, LANES), bf16)] * (2 * chunks)
        + [vmem((BAND, 2, TILE, LANES), bf16)] * chunks
        + [
            vmem((8, LANES), jnp.int32),
            vmem((BAND, 8, LANES), jnp.int32),
            vmem((QUARTERS, TILE, LANES), bf16),
            vmem((BAND, TILE, LANES), bf16),
            vmem((2, BAND, LANES, TILE), bf16),
            vmem((chunks, QUARTERS, LANES, TILE), bf16),
            vmem((chunks, QUARTERS, LANES, TILE), bf16),
        ]
        + [vmem((maxt, 2 * TILE, TILE), f32)] * 2
        + [vmem((2 * TILE, TILE), f32)] * 2
        + [vmem((TILE // LANES, 2 * TILE, LANES), bf16)] * 4
        + [vmem((BAND, LANES, TILE), bf16)]
        + [vmem((maxt + 1, 8, TILE), f32)] * 2
        + [
            vmem((QUARTERS, 8, TILE), f32),
            vmem((maxt + 1, LANES, TILE), f32),
            vmem((maxt + 1, LANES, TILE), f32),
            vmem((maxt + 1, LANES, TILE), f32),
            vmem((chunks, 3, 8, TILE), f32),
            vmem((chunks, far, 3, 8, TILE), f32),
            vmem((chunks, near, 2, LANES, TILE), bf16),
            vmem((chunks, 3, 2, LANES, TILE), bf16),
            vmem((chunks, 2, LANES, TILE), bf16),
            vmem((chunks, 2, 2, LANES, TILE), f32),
            vmem((chunks, QUARTERS, LANES, TILE), bf16),
            vmem((chunks, far, LANES, TILE), bf16),
            vmem((chunks, QUARTERS, LANES, TILE), f32),
            pltpu.SMEM((QUARTERS * BAND,), jnp.int32),
            dma((chunks, 2)),
            dma((chunks, 2)),
            dma((BAND + 1,)),
            dma((chunks, near)),
            dma((chunks, near)),
            dma((chunks, far)),
            dma((chunks, far)),
            dma((chunks, near)),
            dma((chunks, near)),
            dma((chunks, far)),
            dma((chunks, far)),
        ]
    )
    smem = pl.BlockSpec(memory_space=pltpu.SMEM)
    anywhere = pl.BlockSpec(memory_space=pl.ANY)
    results = pl.pallas_call(
        functools.partial(kernel, groups, chunks, maxt),
        out_shape=[jax.ShapeDtypeStruct((rows, width), bf16)] * 3,
        in_specs=[smem, smem] + [anywhere] * 5,
        out_specs=[pl.BlockSpec(memory_space=vmem)] * 3,
        scratch_shapes=scratch,
        compiler_params=pltpu.CompilerParams(
            collective_id=0, has_side_effects=True, vmem_limit_bytes=44 * 1024 * 1024
        ),
    )(
        tile_list,
        tile_count,
        pltpu.with_memory_space_constraint(query_rows.reshape(QUARTERS, TILE, width), pltpu.HBM),
        pltpu.with_memory_space_constraint(key_rows, pltpu.HBM),
        pltpu.with_memory_space_constraint(value_rows, pltpu.HBM),
        pltpu.with_memory_space_constraint(out_grad.reshape(QUARTERS, TILE, width), pltpu.HBM),
        pltpu.with_memory_space_constraint(node_labels.reshape(-1, LANES), pltpu.HBM),
    )
    whole = [pl.BlockSpec(memory_space=vmem)] * 3
    return pl.pallas_call(
        handed_on,
        out_shape=[jax.ShapeDtypeStruct((rows, width), bf16)] * 3,
        in_specs=whole,
        out_specs=whole,
        compiler_params=pltpu.CompilerParams(vmem_limit_bytes=4 * 1024 * 1024),
    )(*results)


def solution(mesh):
    both = P(("dst", "src"), None)
    return jax.shard_map(
        functools.partial(on_device, mesh.shape["dst"]),
        mesh=mesh,
        in_specs=(P("dst", None), both, both, P("dst", None), P(), both, P(("dst", "src"))),
        out_specs=(both, both, both),
        check_vma=False,
    )
```

time: 72.5 us -> 63.2 us (0.87)
  Pallas kernels: 67.5 us -> 61.1 us
  local copies, waits for them, and re-layouts: 3.46 us -> 0.65 us
    pallas_call x1, Pallas kernels: 67.5 us -> 60.2 us  [on_device(): pl.pallas_call(functools.partial(kernel, groups, chunks, maxt), out_shape...]
    unnamed x7 -> x2, local copies, waits for them, and re-layouts: 3.46 us -> 0.65 us
    pallas_call x0 -> x1, Pallas kernels: none -> 0.93 us  [on_device(): pl.pallas_call(handed_on, out_shape=[jax.ShapeDtypeStruct((rows, width),...]
where the time goes in v1:
time: 63.2 us; the launch traced here: 63.1 us
  Pallas kernels  61.1 us (97%)
  between operations  1.3 us (2%)
  local copies, waits for them, and re-layouts  0.65 us (1%)
    pallas_call x1, Pallas kernels, on_device(): pl.pallas_call(functools.partial(kernel, groups, chunks, maxt), out_shape...  60.2 us

profile of v1, /device:TPU:1, one launch (start us, length us, event | category | flops | bytes accessed | tf_op | source)
XLA Modules:
  0.0 63.1 jit_solution(12117048329605791764)
XLA Ops:
  1.3 0.0 copy-start
  1.3 0.6 %copy-done = s32[1,10]{1,0:T(1,128)S(1)} copy-done((s32[1,10]{1,0:T(1,128)S(1)}, s32[1,10]{1,0:T(1,128)}, u32[]{:S(2)}) %copy-start) | copy-done | bytes 64
  1.9 60.2 %shard_map.94 = (bf16[256,512]{1,0:T(8,128)(2,1)S(1)}, bf16[256,512]{1,0:T(8,128)(2,1)S(1)}, bf16[256,512]{1,0:T(8,128)(2,1)S(1)}) custom-call(s32[1,10]{1,0:T(1,128)S(1)} %copy-done, s32[1]{0:T(128)S(6)} %copy.10.refs_1_, bf16[4,256,512]{2,1,0:T(8,128)(2,1)} %bitcast.3, bf16[256,512]{1,0:T(8,128)(2,1)} %refs_3_.1, bf16[256,512]{1,0:T(8,128)(2,1)} %refs_4_.1, ...), custom_call_target="tpu_custom_call" | custom-call | tf_op jit(solution)/shard_map/pallas_call | solution.py:490
  62.2 0.9 %shard_map.95 = (bf16[256,512]{1,0:T(8,128)(2,1)}, bf16[256,512]{1,0:T(8,128)(2,1)}, bf16[256,512]{1,0:T(8,128)(2,1)}) custom-call(bf16[256,512]{1,0:T(8,128)(2,1)S(1)} %get-tuple-element.6.refs_0_, bf16[256,512]{1,0:T(8,128)(2,1)S(1)} %get-tuple-element.7.refs_1_, bf16[256,512]{1,0:T(8,128)(2,1)S(1)} %get-tuple-element.8.refs_2_), custom_call_target="tpu_custom_call" | custom-call | tf_op jit(solution)/shard_map/pallas_call | solution.py:509
Async XLA Ops:
  1.3 0.7 %copy-start = (s32[1,10]{1,0:T(1,128)S(1)}, s32[1,10]{1,0:T(1,128)}, u32[]{:S(2)}) copy-start(s32[1,10]{1,0:T(1,128)} %refs_0_.1) | copy-start | bytes 124

commit v2 on v1

--- a/solution.py
+++ b/solution.py
@@ -186,15 +186,20 @@
         t = lax.div(code, jnp.int32(BAND))
         return t, code - t * BAND
 
-    def score_pass(c):
+    def arrive(c):
         for copy in gathers[c][1:]:
             copy.wait_recv()
+
+    def score_pass(c):
         half = c % 2
-
-        @pl.loop(0, BAND)
-        def _(b):
-            k_t[half, b] = kv_v[c][b, 0].T
-            v_t[b] = kv_v[c][b, 1].T
+        if c < 2:
+            arrive(c)
+
+        if c < 2:
+
+            @pl.loop(0, BAND)
+            def _(b):
+                v_t[half, b] = kv_v[c][b, 1].T
 
         def products(i, odd):
             t, b = entry(i)
@@ -221,13 +226,14 @@
             t, b = entry(i)
             for h in range(2):
                 lanes = pl.ds(h * HEAD_DIM, HEAD_DIM)
-                left = jnp.concatenate([v_t[b, lanes, :], ones], 0)
+                left = jnp.concatenate([v_t[half, b, lanes, :], ones], 0)
                 out = dot(left, joined(pb_v[odd], h), NN)
                 delta = out[:HEAD_DIM] * g_t[c, t, lanes, :].astype(jnp.float32)
                 st_v[half][i, pl.ds(2 + h, 1), :] = out[HEAD_DIM : HEAD_DIM + 1]
                 st_v[half][i, pl.ds(4 + h, 1), :] = jnp.sum(delta, axis=0, keepdims=True)
 
         def visit(n):
+            k_t[half, n] = kv_v[c][n, 0].T
             products(2 * n + 1, 1)
             weigh(2 * n, 0)
             attend(jnp.maximum(2 * n - 1, 0), 1)
@@ -318,6 +324,9 @@
                 dk_c[i, lanes, :] = dot(q_t[c, t, lanes, :], slope, NT)
                 dq_c[i, lanes, :] = dot(k_t[half, b, lanes, :], slope, NN)
 
+        nearing = 2 <= c + 2 < chunks
+        if nearing:
+            arrive(c + 2)
         prob_grads(0, 0)
         prob_grads(1, 1)
         slopes(0, 0)
@@ -325,6 +334,8 @@
         @pl.loop(0, maxt // 2)
         def _(n):
             after = jnp.minimum(2 * n + 2, maxt - 2)
+            if nearing:
+                v_t[half, n] = kv_v[c + 2][n, 1].T
             slopes(2 * n + 1, 1)
             prob_grads(after, 0)
             gradients(2 * n, 0)
@@ -398,7 +409,7 @@
         q_out[:, lanes_of(c)] = total.T.astype(jnp.bfloat16)
 
     stats, grads = {}, {}
-    for c in range(chunks):
+    def turn(c):
         for copy in loads[c]:
             copy.wait()
 
@@ -407,7 +418,12 @@
             q_t[c, t] = q_v[c][t].T
             g_t[c, t] = g_v[c][t].T
 
+    early = chunks // 2
+    for c in range(early):
+        turn(c)
     forward(0)
+    for c in range(early, chunks):
+        turn(c)
     for c in range(chunks + 1):
         if c < chunks:
             stats[c] = score_pass(c)
@@ -455,7 +471,7 @@
         + [vmem((maxt, 2 * TILE, TILE), f32)] * 2
         + [vmem((2 * TILE, TILE), f32)] * 2
         + [vmem((TILE // LANES, 2 * TILE, LANES), bf16)] * 4
-        + [vmem((BAND, LANES, TILE), bf16)]
+        + [vmem((2, BAND, LANES, TILE), bf16)]
         + [vmem((maxt + 1, 8, TILE), f32)] * 2
         + [
             vmem((QUARTERS, 8, TILE), f32),

time: 63.2 us -> 62.5 us (0.989)
  Pallas kernels: 61.1 us -> 60.4 us
    pallas_call x1, Pallas kernels: 60.2 us -> 59.5 us  [on_device(): pl.pallas_call(functools.partial(kernel, groups, chunks, maxt), out_shape...]
where the time goes in v2:
time: 62.5 us; the launch traced here: 62.4 us
  Pallas kernels  60.4 us (97%)
  between operations  1.3 us (2%)
  local copies, waits for them, and re-layouts  0.65 us (1%)
    pallas_call x1, Pallas kernels, on_device(): pl.pallas_call(functools.partial(kernel, groups, chunks, maxt), out_shape...  59.5 us

profile of v2, /device:TPU:1, one launch (start us, length us, event | category | flops | bytes accessed | tf_op | source)
XLA Modules:
  0.0 62.4 jit_solution(10768224608757796576)
XLA Ops:
  1.3 0.0 copy-start
  1.3 0.6 %copy-done = s32[1,10]{1,0:T(1,128)S(1)} copy-done((s32[1,10]{1,0:T(1,128)S(1)}, s32[1,10]{1,0:T(1,128)}, u32[]{:S(2)}) %copy-start) | copy-done | bytes 64
  1.9 59.5 %shard_map.94 = (bf16[256,512]{1,0:T(8,128)(2,1)S(1)}, bf16[256,512]{1,0:T(8,128)(2,1)S(1)}, bf16[256,512]{1,0:T(8,128)(2,1)S(1)}) custom-call(s32[1,10]{1,0:T(1,128)S(1)} %copy-done, s32[1]{0:T(128)S(6)} %copy.10.refs_1_, bf16[4,256,512]{2,1,0:T(8,128)(2,1)} %bitcast.3, bf16[256,512]{1,0:T(8,128)(2,1)} %refs_3_.1, bf16[256,512]{1,0:T(8,128)(2,1)} %refs_4_.1, ...), custom_call_target="tpu_custom_call" | custom-call | tf_op jit(solution)/shard_map/pallas_call | solution.py:506
  61.4 0.9 %shard_map.95 = (bf16[256,512]{1,0:T(8,128)(2,1)}, bf16[256,512]{1,0:T(8,128)(2,1)}, bf16[256,512]{1,0:T(8,128)(2,1)}) custom-call(bf16[256,512]{1,0:T(8,128)(2,1)S(1)} %get-tuple-element.6.refs_0_, bf16[256,512]{1,0:T(8,128)(2,1)S(1)} %get-tuple-element.7.refs_1_, bf16[256,512]{1,0:T(8,128)(2,1)S(1)} %get-tuple-element.8.refs_2_), custom_call_target="tpu_custom_call" | custom-call | tf_op jit(solution)/shard_map/pallas_call | solution.py:525
Async XLA Ops:
  1.3 0.7 %copy-start = (s32[1,10]{1,0:T(1,128)S(1)}, s32[1,10]{1,0:T(1,128)}, u32[]{:S(2)}) copy-start(s32[1,10]{1,0:T(1,128)} %refs_0_.1) | copy-start | bytes 124
